TPU v7x, 512 devices: a whole 4x4x16 slice. The times are simulated.
512 devices in a mesh: section: 4 (over z_hi), dp: 8 (over x, core), tensor: 16 (over z_lo, y).
Axes of the slice: x: 4, y: 4, z: 16 (z_hi: 4, z_lo: 4; z = z_hi * 4 + z_lo), core: 2. Of those that a mesh axis runs over, the one named last changes fastest.
Arguments:
- hidden: bfloat16 [4, 1024, 28672], P('section', 'tensor', 'dp'), may hold values from -6 to 6
- down_weight: bfloat16 [4, 28672, 8192], P('section', 'dp', 'tensor'), may hold values from -0.03125 to 0.03125
- residual: bfloat16 [4, 1024, 8192], P('section', 'dp', 'tensor'), may hold values from -36 to 36
- norm_gain: float32 [4, 8192], P('section', 'tensor'), may hold values from 0.4 to 1.2
- query_weight: bfloat16 [4, 8192, 4096], P('section', 'tensor', 'dp'), may hold values from -0.0625 to 0.0625
- key_value_weight: bfloat16 [4, 8192, 2048], P('section', 'tensor', 'dp'), may hold values from -0.0625 to 0.0625
Outputs:
- attention: bfloat16 [4, 1024, 4096], P('section', 'tensor', 'dp')
All inputs are finite; a program needn't handle non-finite values.
Results may differ from a plain program's by a relative error of at most 0.04.
Values may be sent and summed in bfloat16 or wider, within the bound.
A program may use at most 64 MiB of HBM per device.

v0:
```python
import jax
import jax.numpy as jnp
from jax import lax
from jax.sharding import PartitionSpec as P

D = 8192
HD = 128
ROPE_BASE = 500000.0
EPSILON = 1e-05


def passed_along(value, axis, steps):
    count = lax.axis_size(axis)
    pairs = [(source, (source + steps) % count) for source in range(count)]
    return lax.ppermute(value, axis, pairs)


def rotate(values, positions):
    half_dim = values.shape[-1] // 2
    frequency = ROPE_BASE ** (-jnp.arange(half_dim, dtype=jnp.float32) * 2.0 / values.shape[-1])
    angles = positions.astype(jnp.float32)[:, None] * frequency[None, :]
    cosine = jnp.cos(angles)[:, None, :]
    sine_part = jnp.sin(angles)[:, None, :]
    front_part = values[..., :half_dim]
    back_part = values[..., half_dim:]
    return jnp.concatenate(
        [front_part * cosine - back_part * sine_part, back_part * cosine + front_part * sine_part],
        axis=-1,
    )


def per_device(hidden, down_weight, residual, norm_gain, query_weight, key_value_weight):
    weight_block = down_weight[0]
    partials = jnp.dot(
        lax.all_gather(hidden[0], "tensor", axis=0, tiled=True),
        weight_block,
        preferred_element_type=jnp.float32,
    )
    summed = lax.psum_scatter(
        partials.astype(jnp.bfloat16), "dp", scatter_dimension=0, tiled=True
    ).astype(jnp.float32)
    boundary = (residual[0].astype(jnp.float32) + summed).astype(jnp.bfloat16)
    gathered = lax.all_gather(boundary, "dp", axis=0, tiled=True)
    arrived = passed_along(gathered, "section", 1)
    values_in = arrived.astype(jnp.float32)
    squares = jnp.sum(values_in * values_in, axis=1)
    scaled = (values_in * norm_gain[0][None, :]).astype(jnp.bfloat16)
    query_sums = jnp.dot(scaled, query_weight[0], preferred_element_type=jnp.float32)
    pair_sums = jnp.dot(scaled, key_value_weight[0], preferred_element_type=jnp.float32)
    token_count = arrived.shape[0]
    own_rows = token_count // lax.axis_size("tensor")
    first_row = lax.axis_index("tensor") * own_rows
    query_sums, pair_sums, squares = (
        lax.psum(query_sums.astype(jnp.bfloat16), "tensor").astype(jnp.float32),
        lax.psum(pair_sums.astype(jnp.bfloat16), "tensor").astype(jnp.float32),
        lax.psum(squares.astype(jnp.bfloat16), "tensor").astype(jnp.float32),
    )
    query_local = lax.dynamic_slice_in_dim(query_sums, first_row, own_rows, 0)
    inverse = lax.rsqrt(squares / D + EPSILON)[:, None]
    positions = jnp.arange(token_count, dtype=jnp.int32)
    own_positions = first_row + jnp.arange(own_rows, dtype=jnp.int32)
    inverse_own = lax.dynamic_slice_in_dim(inverse, first_row, own_rows, 0)
    query_part = query_local * inverse_own
    queries = rotate(query_part.reshape(own_rows, -1, HD), own_positions).astype(jnp.bfloat16)
    pair_rows = (pair_sums * inverse).reshape(token_count, -1, 2, HD)
    key_rows = rotate(pair_rows[:, :, 0], positions).astype(jnp.bfloat16)
    value_rows = pair_rows[:, :, 1].astype(jnp.bfloat16)
    group_count = key_rows.shape[1]
    grouped = queries.reshape(own_rows, group_count, -1, HD)
    scores = jnp.einsum(
        "qgrd,kgd->grqk", grouped, key_rows, preferred_element_type=jnp.float32
    ) * HD ** (-0.5)
    causal = positions[None, :] <= own_positions[:, None]
    scores = jnp.where(causal[None, None], scores, -1e30)
    maximum = jnp.max(scores, axis=-1, keepdims=True)
    weights = jnp.exp(scores - maximum)
    probabilities = (weights / jnp.sum(weights, axis=-1, keepdims=True)).astype(jnp.bfloat16)
    attended = jnp.einsum(
        "grqk,kgd->qgrd", probabilities, value_rows, preferred_element_type=jnp.float32
    ).astype(jnp.bfloat16)
    return attended.reshape(own_rows, -1)[None]


def solution(mesh):
    placed = (
        P("section", "tensor", "dp"),
        P("section", "dp", "tensor"),
        P("section", "dp", "tensor"),
        P("section", "tensor"),
        P("section", "tensor", "dp"),
        P("section", "tensor", "dp"),
    )
    return jax.shard_map(
        per_device,
        mesh=mesh,
        in_specs=placed,
        out_specs=P("section", "tensor", "dp"),
        check_vma=False,
    )
```

profile of v0, /device:TPU:2, one launch (start us, length us, event | category | flops | bytes accessed | tf_op | source)
XLA Modules:
  0.0 486.2 jit_solution(7943351588400073942)
XLA Ops:
  6.5 0.0 copy-start
  6.5 0.0 all-gather.6.cloned.1.call-start
  6.5 0.7 all-gather.6.cloned.1.call-update
  7.3 0.0 copy-start.1
  7.3 0.0 copy-start.2
  7.3 0.0 copy-start.3
  7.3 0.0 reduce-scatter.2.cloned.1.call-start
  7.3 108.6 %all-gather.6.cloned.1.call-done = bf16[1,1024,3584]{2,1,0:T(8,128)(2,1)} async-done(((bf16[1,64,3584]{2,1,0:T(8,128)(2,1)}), bf16[1,1024,3584]{2,1,0:T(8,128)(2,1)}) %all-gather.6.cloned.1.call-update) | async-done | bytes 7340048 | tf_op jit(solution)/shard_map/all_gather | solution.py:35
  115.9 9.1 %fusion.5 = bf16[1024,512]{1,0:T(8,128)(2,1)} fusion(bf16[1,3584,512]{2,1,0:T(8,128)(2,1)} %param.7, bf16[1,1024,3584]{2,1,0:T(8,128)(2,1)} %all-gather.6.cloned.1.call-done), kind=kOutput, calls=%fused_computation.7 | convolution fusion | flops 3758620672 | bytes 12058624 | tf_op jit(solution)/shard_map/dot_general | solution.py:34
  125.0 0.0 reduce-scatter.2.cloned.1.call-update
  125.0 0.0 all-gather.4.cloned.1.call-start
  125.0 33.0 %reduce-scatter.2.cloned.1.call-done = bf16[128,512]{1,0:T(8,128)(2,1)} async-done(((bf16[1024,512]{1,0:T(8,128)(2,1)}), bf16[128,512]{1,0:T(8,128)(2,1)}) %reduce-scatter.2.cloned.1.call-update) | async-done | bytes 131088 | tf_op jit(solution)/shard_map/reduce_scatter | solution.py:39
  158.0 0.0 copy-done.1
  158.0 1.6 fusion.30
  159.6 0.0 all-gather.4.cloned.1.call-update
  159.6 0.0 all-reduce.3.cloned.1.call-start
  159.7 32.3 %all-gather.4.cloned.1.call-done = bf16[1024,512]{1,0:T(8,128)(2,1)} async-done(((bf16[128,512]{1,0:T(8,128)(2,1)}), bf16[1024,512]{1,0:T(8,128)(2,1)}) %all-gather.4.cloned.1.call-update) | async-done | bytes 1048592 | tf_op jit(solution)/shard_map/all_gather | solution.py:43
  192.0 7.2 %collective-permute-start = (bf16[1024,512]{1,0:T(8,128)(2,1)}, bf16[1024,512]{1,0:T(8,128)(2,1)S(1)}, u32[]{:S(2)}, u32[]{:S(2)}) collective-permute-start(bf16[1024,512]{1,0:T(8,128)(2,1)} %all-gather.4.cloned.1.call-done), channel_id=1, source_target_pairs={{0,128},{128,256},{256,384},{384,0},{1,129},{129,257},{257,385},{3... | collective-permute-start | bytes 3145736 | tf_op jit(solution)/shard_map/ppermute | solution.py:15
  199.2 55.4 %collective-permute-done = bf16[1024,512]{1,0:T(8,128)(2,1)S(1)} collective-permute-done((bf16[1024,512]{1,0:T(8,128)(2,1)}, bf16[1024,512]{1,0:T(8,128)(2,1)S(1)}, u32[]{:S(2)}, u32[]{:S(2)}) %collective-permute-start) | collective-permute-done | bytes 1048608 | tf_op jit(solution)/shard_map/ppermute | solution.py:15
  254.6 0.0 copy-done.2
  254.6 0.0 copy-done.3
  254.6 1.3 convolution_convert_fusion.1
  255.8 0.0 copy-done
  255.8 1.8 convolution_convert_fusion
  257.6 0.0 all-reduce.3.cloned.1.call-update
  257.7 0.1 iota_compare_fusion
  257.8 0.2 multiply_cosine_fusion.1
  258.0 0.3 fusion.4
  258.2 79.6 %psum.22 = bf16[1024]{0:T(1024)(128)(2,1)S(1)} all-reduce(bf16[1024]{0:T(1024)(128)(2,1)S(1)} %fusion.4), channel_id=1, replica_groups=mesh['section'=4,'dp'=8,'tensor'=16] {'tensor'}, use_global_device_ids=true, to_apply=%region_3.0 | all-reduce | flops 1024 | bytes 4096 | tf_op jit(solution)/shard_map/psum | solution.py:56
  337.8 0.1 dynamic-slice.3
  337.9 133.5 %all-reduce.3.cloned.1.call-done = (bf16[1024,256]{1,0:T(8,128)(2,1)}, bf16[1024,512]{1,0:T(8,128)(2,1)}) async-done(((bf16[1024,256]{1,0:T(8,128)(2,1)}, bf16[1024,512]{1,0:T(8,128)(2,1)}), (bf16[1024,256]{1,0:T(8,128)(2,1)}, bf16[1024,512]{1,0:T(8,128)(2,1)})) %all-reduce.3.cloned.1.call-update) | async-done | bytes 1572880 | tf_op jit(solution)/shard_map/psum | solution.py:55
  471.5 1.2 convert_multiply_fusion.2
  472.7 0.5 reshape.223
  473.3 0.4 slice.26
  473.6 0.5 slice.25
  474.2 0.9 convert_multiply_fusion.3
  475.2 0.1 fusion.39
  475.3 2.4 fusion.33
  477.8 0.5 fusion.40
  478.3 0.3 fusion.13
  478.6 0.4 fusion.12
  479.0 0.1 copy.15
  479.1 0.7 broadcast_in_dim_reshape.3
  (7 shorter events, 0.2 us)
Async XLA Ops:
  6.5 249.3 %copy-start = (bf16[1,512,512]{2,1,0:T(8,128)(2,1)S(1)}, bf16[1,512,512]{2,1,0:T(8,128)(2,1)}, u32[]{:S(2)}) copy-start(bf16[1,512,512]{2,1,0:T(8,128)(2,1)} %param.10) | copy-start | bytes 1572868
  6.5 109.4 %all-gather.6.cloned.1.call-start = ((), (), s32[]{:S(2)}) async-start(), calls=%async_computation.3 | async-start | bytes 7798784 | tf_op jit(solution)/shard_map/all_gather | solution.py:35
  7.3 150.7 %copy-start.1 = (bf16[1,128,512]{2,1,0:T(8,128)(2,1)S(1)}, bf16[1,128,512]{2,1,0:T(8,128)(2,1)}, u32[]{:S(2)}) copy-start(bf16[1,128,512]{2,1,0:T(8,128)(2,1)} %param.8) | copy-start | bytes 393220
  7.3 247.3 %copy-start.2 = (bf16[1,512,256]{2,1,0:T(8,128)(2,1)S(1)}, bf16[1,512,256]{2,1,0:T(8,128)(2,1)}, u32[]{:S(2)}) copy-start(bf16[1,512,256]{2,1,0:T(8,128)(2,1)} %param.11) | copy-start | bytes 786436
  7.3 247.3 %copy-start.3 = (f32[1,512]{1,0:T(1,128)S(1)}, f32[1,512]{1,0:T(1,128)}, u32[]{:S(2)}) copy-start(f32[1,512]{1,0:T(1,128)} %param.9) | copy-start | bytes 6148
  7.3 150.7 %reduce-scatter.2.cloned.1.call-start = ((), (), s32[]{:S(2)}) async-start(), calls=%async_computation.1 | async-start | bytes 1179648 | tf_op jit(solution)/shard_map/reduce_scatter | solution.py:39
  125.0 67.0 %all-gather.4.cloned.1.call-start = ((), (), s32[]{:S(2)}) async-start(), calls=%async_computation.2 | async-start | bytes 1179648 | tf_op jit(solution)/shard_map/all_gather | solution.py:43
  159.6 311.9 %all-reduce.3.cloned.1.call-start = ((), (), s32[]{:S(2)}) async-start(), calls=%async_computation.4 | async-start | bytes 3145728 | tf_op jit(solution)/shard_map/psum | solution.py:55
  192.0 62.6 %collective-permute-start = (bf16[1024,512]{1,0:T(8,128)(2,1)}, bf16[1024,512]{1,0:T(8,128)(2,1)S(1)}, u32[]{:S(2)}, u32[]{:S(2)}) collective-permute-start(bf16[1024,512]{1,0:T(8,128)(2,1)} %all-gather.4.cloned.1.call-done), channel_id=1, source_target_pairs={{0,128},{128,256},{256,384},{384,0},{1,129},{129,257},{257,385},{3... | collective-permute-start | bytes 3145736 | tf_op jit(solution)/shard_map/ppermute | solution.py:15
Sparse Core Ops, SparseCore 0:
  9.4 106.4 all-gather.5
  125.1 32.8 reduce-scatter.1
  160.1 31.7 all-gather.3
  257.7 213.6 all-reduce.2
where the time goes:
time: 486 us
  waiting for transfers between devices  364 us (75%)
  blocking collectives  79.6 us (16%)
  between operations  13.3 us (3%)
  matrix products  12.9 us (3%)
  starting transfers between devices  7.32 us (2%)
  other arithmetic  7.13 us (1%)
    psum x1, waiting for transfers between devices, per_device(): lax.psum(pair_sums.astype(jnp.bfloat16), 'tensor').astype(jnp.float32)  134 us
    all_gather x1, waiting for transfers between devices, per_device(): lax.all_gather(hidden[0], 'tensor', axis=0, tiled=True)  109 us
    psum x1, blocking collectives, per_device(): lax.psum(squares.astype(jnp.bfloat16), 'tensor').astype(jnp.float32)  79.6 us
    ppermute x1, waiting for transfers between devices, passed_along(): return lax.ppermute(value, axis, pairs)  55.4 us
    reduce_scatter x1, waiting for transfers between devices, per_device(): lax.psum_scatter(partials.astype(jnp.bfloat16), 'dp', scatter_dimension=0...  33 us
    all_gather x1, waiting for transfers between devices, per_device(): gathered = lax.all_gather(boundary, 'dp', axis=0, tiled=True)  32.3 us
  transfers between devices with their start and end apart: 5, of which 5 were waited for; matrix products, arithmetic and copies ran while one was open for 0% of the time, Pallas kernels for 0%

commit v1 on v0

--- a/solution.py
+++ b/solution.py
@@ -7,6 +7,10 @@
 HD = 128
 ROPE_BASE = 500000.0
 EPSILON = 1e-05
+
+
+def press_sums_all(field_in):
+    return jnp.sum(lax.all_gather(field_in, axis_name="tensor"), 0)
 
 
 def passed_along(value, axis, steps):
@@ -52,7 +56,7 @@
     first_row = lax.axis_index("tensor") * own_rows
     query_sums, pair_sums, squares = (
         lax.psum(query_sums.astype(jnp.bfloat16), "tensor").astype(jnp.float32),
-        lax.psum(pair_sums.astype(jnp.bfloat16), "tensor").astype(jnp.float32),
+        press_sums_all(pair_sums.astype(jnp.bfloat16)).astype(jnp.float32),
         lax.psum(squares.astype(jnp.bfloat16), "tensor").astype(jnp.float32),
     )
     query_local = lax.dynamic_slice_in_dim(query_sums, first_row, own_rows, 0)

time: 486 us -> 594 us (1.22)
  the two profiles are of different devices: /device:TPU:2 before, /device:TPU:1 now
where the time goes in v1:
time: 594 us; the launch traced here: 593 us
  waiting for transfers between devices  474 us (80%)
  blocking collectives  73.4 us (12%)
  between operations  13.3 us (2%)
  matrix products  12.9 us (2%)
  other arithmetic  10.9 us (2%)
  starting transfers between devices  7.35 us (1%)
    psum x1, waiting for transfers between devices, per_device(): lax.psum(query_sums.astype(jnp.bfloat16), 'tensor').astype(jnp.float32)  124 us
    all_gather x1, waiting for transfers between devices, press_sums_all(): return jnp.sum(lax.all_gather(field_in, axis_name='tensor'), 0)  117 us
    all_gather x1, waiting for transfers between devices, per_device(): lax.all_gather(hidden[0], 'tensor', axis=0, tiled=True)  103 us
    psum x1, blocking collectives, per_device(): lax.psum(squares.astype(jnp.bfloat16), 'tensor').astype(jnp.float32)  73.4 us
    ppermute x1, waiting for transfers between devices, passed_along(): return lax.ppermute(value, axis, pairs)  55.1 us
    reduce_scatter x1, waiting for transfers between devices, per_device(): lax.psum_scatter(partials.astype(jnp.bfloat16), 'dp', scatter_dimension=0...  40.9 us
    all_gather x1, waiting for transfers between devices, per_device(): gathered = lax.all_gather(boundary, 'dp', axis=0, tiled=True)  32.7 us
  transfers between devices with their start and end apart: 6, of which 6 were waited for; matrix products, arithmetic and copies ran while one was open for 1% of the time, Pallas kernels for 0%

profile of v1, /device:TPU:1, one launch (start us, length us, event | category | flops | bytes accessed | tf_op | source)
XLA Modules:
  0.0 593.3 jit_solution(13348854013623134467)
XLA Ops:
  6.5 0.0 copy-start
  6.5 0.0 all-gather.8.cloned.1.call-start
  6.5 0.7 all-gather.8.cloned.1.call-update
  7.3 0.0 copy-start.1
  7.3 0.0 copy-start.3
  7.3 0.0 reduce-scatter.2.cloned.1.call-start
  7.3 102.9 %all-gather.8.cloned.1.call-done = bf16[1,1024,3584]{2,1,0:T(8,128)(2,1)} async-done(((bf16[1,64,3584]{2,1,0:T(8,128)(2,1)}), bf16[1,1024,3584]{2,1,0:T(8,128)(2,1)}) %all-gather.8.cloned.1.call-update) | async-done | bytes 7340048 | tf_op jit(solution)/shard_map/all_gather | solution.py:39
  110.2 9.1 %fusion.5 = bf16[1024,512]{1,0:T(8,128)(2,1)} fusion(bf16[1,3584,512]{2,1,0:T(8,128)(2,1)} %param.7, bf16[1,1024,3584]{2,1,0:T(8,128)(2,1)} %all-gather.8.cloned.1.call-done), kind=kOutput, calls=%fused_computation.7 | convolution fusion | flops 3758620672 | bytes 12058624 | tf_op jit(solution)/shard_map/dot_general | solution.py:38
  119.2 0.0 reduce-scatter.2.cloned.1.call-update
  119.3 0.0 all-gather.6.cloned.1.call-start
  119.3 40.9 %reduce-scatter.2.cloned.1.call-done = bf16[128,512]{1,0:T(8,128)(2,1)} async-done(((bf16[1024,512]{1,0:T(8,128)(2,1)}), bf16[128,512]{1,0:T(8,128)(2,1)}) %reduce-scatter.2.cloned.1.call-update) | async-done | bytes 131088 | tf_op jit(solution)/shard_map/reduce_scatter | solution.py:43
  160.3 0.0 copy-done.1
  160.3 1.6 fusion.30
  161.8 0.0 all-gather.6.cloned.1.call-update
  161.9 0.0 all-reduce.2.cloned.1.call-start
  161.9 32.7 %all-gather.6.cloned.1.call-done = bf16[1024,512]{1,0:T(8,128)(2,1)} async-done(((bf16[128,512]{1,0:T(8,128)(2,1)}), bf16[1024,512]{1,0:T(8,128)(2,1)}) %all-gather.6.cloned.1.call-update) | async-done | bytes 1048592 | tf_op jit(solution)/shard_map/all_gather | solution.py:47
  194.6 7.2 %collective-permute-start = (bf16[1024,512]{1,0:T(8,128)(2,1)}, bf16[1024,512]{1,0:T(8,128)(2,1)S(1)}, u32[]{:S(2)}, u32[]{:S(2)}) collective-permute-start(bf16[1024,512]{1,0:T(8,128)(2,1)} %all-gather.6.cloned.1.call-done), channel_id=1, source_target_pairs={{0,128},{128,256},{256,384},{384,0},{1,129},{129,257},{257,385},{3... | collective-permute-start | bytes 3145736 | tf_op jit(solution)/shard_map/ppermute | solution.py:19
  201.8 55.1 %collective-permute-done = bf16[1024,512]{1,0:T(8,128)(2,1)S(1)} collective-permute-done((bf16[1024,512]{1,0:T(8,128)(2,1)}, bf16[1024,512]{1,0:T(8,128)(2,1)S(1)}, u32[]{:S(2)}, u32[]{:S(2)}) %collective-permute-start) | collective-permute-done | bytes 1048608 | tf_op jit(solution)/shard_map/ppermute | solution.py:19
  256.9 0.0 copy-done
  256.9 0.0 copy-done.3
  256.9 0.0 copy-start.2
  256.9 1.7 convolution_convert_fusion
  258.6 0.0 all-reduce.2.cloned.1.call-update
  258.6 0.0 all-gather.10.cloned.1.call-start
  258.7 0.0 copy-done.2
  258.7 1.3 convolution_convert_fusion.1
  259.9 0.0 all-gather.10.cloned.1.call-update
  260.0 0.1 iota_compare_fusion
  260.1 0.2 multiply_cosine_fusion.1
  260.3 0.3 fusion.4
  260.6 73.4 %psum.14 = bf16[1024]{0:T(1024)(128)(2,1)S(1)} all-reduce(bf16[1024]{0:T(1024)(128)(2,1)S(1)} %fusion.4), channel_id=1, replica_groups=mesh['section'=4,'dp'=8,'tensor'=16] {'tensor'}, use_global_device_ids=true, to_apply=%region_3.0 | all-reduce | flops 1024 | bytes 4096 | tf_op jit(solution)/shard_map/psum | solution.py:60
  334.0 0.1 dynamic-slice.3
  334.0 124.3 %all-reduce.2.cloned.1.call-done = bf16[1024,512]{1,0:T(8,128)(2,1)} async-done(((bf16[1024,512]{1,0:T(8,128)(2,1)}), bf16[1024,512]{1,0:T(8,128)(2,1)}) %all-reduce.2.cloned.1.call-update) | async-done | bytes 1048592 | tf_op jit(solution)/shard_map/psum | solution.py:58
  458.4 0.9 convert_multiply_fusion.2
  459.4 0.1 fusion.39
  459.5 117.3 %all-gather.10.cloned.1.call-done = bf16[16384,256]{1,0:T(8,128)(2,1)} async-done(((bf16[1024,256]{1,0:T(8,128)(2,1)}), bf16[16384,256]{1,0:T(8,128)(2,1)}) %all-gather.10.cloned.1.call-update) | async-done | bytes 8388624 | tf_op jit(solution)/shard_map/all_gather | solution.py:13
  576.8 4.8 reduce_sum.30
  581.6 0.2 copy.13
  581.8 0.3 copy.14
  582.2 0.2 broadcast_multiply_fusion
  582.4 2.4 fusion.33
  584.9 0.5 fusion.40
  585.3 0.3 fusion.13
  585.7 0.4 fusion.12
  586.0 0.1 copy.17
  586.1 0.7 broadcast_in_dim_reshape.3
  (7 shorter events, 0.2 us)
Async XLA Ops:
  6.5 250.4 %copy-start = (bf16[1,512,512]{2,1,0:T(8,128)(2,1)S(1)}, bf16[1,512,512]{2,1,0:T(8,128)(2,1)}, u32[]{:S(2)}) copy-start(bf16[1,512,512]{2,1,0:T(8,128)(2,1)} %param.10) | copy-start | bytes 1572868
  6.5 103.6 %all-gather.8.cloned.1.call-start = ((), (), s32[]{:S(2)}) async-start(), calls=%async_computation.4 | async-start | bytes 7798784 | tf_op jit(solution)/shard_map/all_gather | solution.py:39
  7.3 153.0 %copy-start.1 = (bf16[1,128,512]{2,1,0:T(8,128)(2,1)S(1)}, bf16[1,128,512]{2,1,0:T(8,128)(2,1)}, u32[]{:S(2)}) copy-start(bf16[1,128,512]{2,1,0:T(8,128)(2,1)} %param.8) | copy-start | bytes 393220
  7.3 249.6 %copy-start.3 = (f32[1,512]{1,0:T(1,128)S(1)}, f32[1,512]{1,0:T(1,128)}, u32[]{:S(2)}) copy-start(f32[1,512]{1,0:T(1,128)} %param.9) | copy-start | bytes 6148
  7.3 153.0 %reduce-scatter.2.cloned.1.call-start = ((), (), s32[]{:S(2)}) async-start(), calls=%async_computation.1 | async-start | bytes 1179648 | tf_op jit(solution)/shard_map/reduce_scatter | solution.py:43
  119.3 75.4 %all-gather.6.cloned.1.call-start = ((), (), s32[]{:S(2)}) async-start(), calls=%async_computation.2 | async-start | bytes 1179648 | tf_op jit(solution)/shard_map/all_gather | solution.py:47
  161.9 296.5 %all-reduce.2.cloned.1.call-start = ((), (), s32[]{:S(2)}) async-start(), calls=%async_computation.3 | async-start | bytes 2097152 | tf_op jit(solution)/shard_map/psum | solution.py:58
  194.6 62.3 %collective-permute-start = (bf16[1024,512]{1,0:T(8,128)(2,1)}, bf16[1024,512]{1,0:T(8,128)(2,1)S(1)}, u32[]{:S(2)}, u32[]{:S(2)}) collective-permute-start(bf16[1024,512]{1,0:T(8,128)(2,1)} %all-gather.6.cloned.1.call-done), channel_id=1, source_target_pairs={{0,128},{128,256},{256,384},{384,0},{1,129},{129,257},{257,385},{3... | collective-permute-start | bytes 3145736 | tf_op jit(solution)/shard_map/ppermute | solution.py:19
  256.9 1.8 copy-start.2
  258.6 318.2 %all-gather.10.cloned.1.call-start = ((), (), s32[]{:S(2)}) async-start(), calls=%async_computation.5 | async-start | bytes 8912896 | tf_op jit(solution)/shard_map/all_gather | solution.py:13
Sparse Core Ops, SparseCore 0:
  9.4 100.6 all-gather.7
  119.4 40.8 reduce-scatter.1
  162.4 32.1 all-gather.5
  258.7 199.5 all-reduce.1
  460.5 116.2 all-gather.9
